TPU v7x, 256 devices: a whole 4x4x8 slice. The times are simulated.
256 devices in a mesh: blk: 16 (over z, x_hi), leaf: 8 (over y, core), rhs: 2 (over x_lo).
Axes of the slice: x: 4 (x_hi: 2, x_lo: 2; x = x_hi * 2 + x_lo), y: 4, z: 8, core: 2. Of those that a mesh axis runs over, the one named last changes fastest.
Arguments:
- residual: float32 [32, 8, 65536], P('rhs', 'leaf', 'blk'), may hold values from -160 to 160
- points: float32 [3, 8, 65536], P(None, 'leaf', 'blk'), may hold values from -12330 to 12330
- noise: float32 [8, 65536], P('leaf', 'blk'), may hold values from 1 to 2
- block_list: int32 [8, 8, 256], P('leaf'), may hold values from 0 to 1, as said below
Outputs:
- correction: float32 [32, 8, 65536], P('rhs', 'leaf', 'blk')
- new_residual: float32 [32, 8, 65536], P('rhs', 'leaf', 'blk')
- basis: float32 [128, 8, 65536], P('rhs', 'leaf', 'blk')
Inputs may be any that keep to these rules, and one draw needn't show every extreme that they name: The list is symmetric: block_list[t, k, i] == block_list[t, 7 - k, (i + d) mod 256] with d the offset of entry k.
All inputs are finite; a program needn't handle non-finite values.
Results may differ from a plain program's by a relative error of at most 0.007.
Values sent between devices are 32-bit elements; how exact they have to be, the bound alone decides.
A program may use at most 128 MiB of HBM per device.

v0:
```python
import jax
import jax.numpy as jnp
from jax import lax
from jax.sharding import PartitionSpec as P

M = 32
S = 4
BS = 256
REACH = 4
SUPPORT = 1408
centre_shift = 1.5
amplitude = 1.1
exact = lax.Precision.HIGHEST


def extended(x, sides, width):
    for axis, dim in sides:
        count, length = (lax.axis_size(axis), x.shape[dim])
        up = [(i, (i + 1) % count) for i in range(count)]
        down = [(j, i) for i, j in up]
        last = lax.slice_in_dim(x, length - width, length, axis=dim)
        leading = lax.slice_in_dim(x, 0, width, axis=dim)
        before = lax.ppermute(last, axis, up)
        after = lax.ppermute(leading, axis, down)
        x = jnp.concatenate([before, x, after], axis=dim)
    return x


def kernel_tile(near_points, own_points):
    squared = (near_points[0][:, None] - own_points[0][None, :]) ** 2
    squared = squared + (near_points[1][:, None] - own_points[1][None, :]) ** 2
    squared = squared + (near_points[2][:, None] - own_points[2][None, :]) ** 2
    radius = jnp.sqrt(squared) / SUPPORT
    remain = jnp.maximum(1.0 - radius, 0.0)
    return remain * remain * (remain * remain) * (4.0 * radius + 1.0) * (amplitude / SUPPORT)


def band_product(field_wide, points_wide, weights, rows_out):
    per_turn = rows_out // 8
    count = field_wide.shape[0]

    def turn(carry, index):
        pieces = []
        for inner in range(per_turn):
            block = index * per_turn + inner
            own_points = lax.dynamic_slice_in_dim(points_wide, (block + REACH) * BS, BS, 1)
            total = jnp.zeros((count, BS), jnp.float32)
            for offset in range(2 * REACH + 1):
                column_at = (block + offset) * BS
                near_points = lax.dynamic_slice_in_dim(points_wide, column_at, BS, 1)
                near_field = lax.dynamic_slice_in_dim(field_wide, column_at, BS, 1)
                listed = lax.dynamic_index_in_dim(weights[offset], block, 0, False)
                tile = kernel_tile(near_points, own_points) * listed
                total = total + jnp.dot(near_field, tile, precision=exact)
            pieces.append(total)
        return (carry, jnp.concatenate(pieces, axis=1))

    carry, parts = lax.scan(turn, jnp.zeros((), jnp.int32), jnp.arange(8, dtype=jnp.int32))
    return jnp.moveaxis(parts, 0, 1).reshape(count, rows_out * BS)


def galerkin(gram, count_points, count_sides):
    normed = gram / count_points
    basis_count = normed.shape[0] - count_sides
    gram_basis = normed[:basis_count, :basis_count]
    factor_low = jnp.linalg.cholesky(gram_basis)
    inverse_low = lax.linalg.triangular_solve(
        factor_low, jnp.eye(basis_count, dtype=jnp.float32), left_side=True, lower=True
    )
    cross = normed[:basis_count, count_sides:] + centre_shift * gram_basis
    projected = jnp.dot(
        jnp.dot(inverse_low, cross, precision=exact), inverse_low.T, precision=exact
    )
    projected = 0.5 * (projected + projected.T)
    small_side = jnp.dot(inverse_low, gram_basis[:, :count_sides], precision=exact)
    proj_factor = jnp.linalg.cholesky(projected)
    halfway = lax.linalg.triangular_solve(proj_factor, small_side, left_side=True, lower=True)
    coeffs = lax.linalg.triangular_solve(
        proj_factor, halfway, left_side=True, lower=True, transpose_a=True
    )
    combo = jnp.dot(coeffs.T, inverse_low, precision=exact)
    return (inverse_low, combo)


def row_products(rows):
    return lax.dot_general(rows, rows, (((1,), (1,)), ((), ())), precision=exact)


def local(residual, points, noise, block_list):
    field = residual[:, 0]
    coords = points[:, 0]
    nugget = noise[0]
    own_rows = field.shape[1]
    own_blocks = own_rows // BS
    first_block = lax.axis_index("blk") * own_blocks
    listed = block_list[0].astype(jnp.float32)
    nine = jnp.concatenate(
        [listed[:REACH], jnp.ones((1, listed.shape[1]), jnp.float32), listed[REACH:]], axis=0
    )
    margin = S * REACH
    wrapped = jnp.concatenate([nine[:, -margin:], nine, nine[:, :margin]], axis=1)
    powers = [field]
    rim = REACH * BS
    coords_wide = extended(coords, (("blk", 1),), rim)
    own_weights = lax.dynamic_slice_in_dim(wrapped, first_block + margin, own_blocks, 1)
    current = field
    for power_step in range(S):
        widened = extended(current, (("blk", 1),), rim)
        current = (
            band_product(widened, coords_wide, own_weights, own_blocks)
            + (nugget - centre_shift) * current
        )
        powers.append(current)
    half_panel = jnp.stack(powers, axis=0)
    count_points = own_rows * lax.axis_size("blk") * lax.axis_size("leaf")
    sides_here = field.shape[0]
    whole = lax.all_gather(half_panel, "rhs", axis=1, tiled=True)
    flat = whole.reshape(-1, own_rows)
    gram = lax.psum(row_products(flat), ("blk", "leaf"))
    inverse_low, combo = galerkin(gram, count_points, M)
    first_rows = flat[: S * M]
    image = flat[M:] + centre_shift * first_rows
    part = lax.axis_index("rhs")
    basis_here = S * M // lax.axis_size("rhs")
    mine_low = lax.dynamic_slice_in_dim(inverse_low, part * basis_here, basis_here, 0)
    mine_combo = lax.dynamic_slice_in_dim(combo, part * sides_here, sides_here, 0)
    correction = jnp.dot(mine_combo, first_rows, precision=exact)
    new_residual = field - jnp.dot(mine_combo, image, precision=exact)
    basis = jnp.dot(mine_low, first_rows, precision=exact)
    return (correction[:, None], new_residual[:, None], basis[:, None])


def solution(mesh):
    placed = (
        P("rhs", "leaf", "blk"),
        P(None, "leaf", "blk"),
        P("leaf", "blk"),
        P("leaf", None, None),
    )
    return jax.shard_map(
        local,
        mesh=mesh,
        in_specs=placed,
        out_specs=(P("rhs", "leaf", "blk"), P("rhs", "leaf", "blk"), P("rhs", "leaf", "blk")),
        check_vma=False,
    )
```

profile of v0, /device:TPU:2, one launch (start us, length us, event | category | flops | bytes accessed | tf_op | source)
XLA Modules:
  0.0 2114.2 jit_solution(17787421845742051918)
XLA Ops:
  8.1 2.2 collective-permute-start.2
  10.3 5.4 collective-permute-start.3
  15.6 1.1 copy.47
  16.9 5.6 collective-permute-start.1
  22.5 1.1 bitcast_dynamic-update-slice_fusion
  25.4 206.0 %while.52 = (s32[]{:T(128)}, f32[8,16,512]{2,1,0:T(8,128)S(1)}, s32[8]{0:T(128)S(1)}, f32[16,6144]{1,0:T(8,128)S(1)}, f32[3,6144]{1,0:T(4,128)S(1)}, /*index=5*/...) while((s32[]{:T(128)}, f32[8,16,512]{2,1,0:T(8,128)S(1)}, ...), condition=%wide.region_1.2_spmd, body=%wide.region_0.1_spmd.sunk | while | flops 246620224 | bytes 1092197 | solution.py:58
  231.9 5.6 collective-permute-start.5
  237.9 1.8 collective-permute-done.4
  239.8 202.8 %while.53 = (s32[]{:T(128)}, f32[8,16,512]{2,1,0:T(8,128)S(1)}, s32[8]{0:T(128)S(1)}, f32[16,6144]{1,0:T(8,128)S(1)}, f32[3,6144]{1,0:T(4,128)S(1)}, /*index=5*/...) while((s32[]{:T(128)}, f32[8,16,512]{2,1,0:T(8,128)S(1)}, ...), condition=%wide.region_3.4_spmd, body=%wide.region_2.3_spmd.sunk | while | flops 246620224 | bytes 1092197 | solution.py:58
  442.8 6.1 collective-permute-start.7
  449.2 1.5 collective-permute-done.6
  450.9 203.8 %while.54 = (s32[]{:T(128)}, f32[8,16,512]{2,1,0:T(8,128)S(1)}, s32[8]{0:T(128)S(1)}, f32[16,6144]{1,0:T(8,128)S(1)}, f32[3,6144]{1,0:T(4,128)S(1)}, /*index=5*/...) while((s32[]{:T(128)}, f32[8,16,512]{2,1,0:T(8,128)S(1)}, ...), condition=%wide.region_5.6_spmd, body=%wide.region_4.5_spmd.sunk | while | flops 246620224 | bytes 1092197 | solution.py:58
  654.8 1.9 collective-permute-start.8
  656.7 4.4 collective-permute-start.9
  661.4 1.8 collective-permute-done.8
  663.4 207.7 %while.55 = (s32[]{:T(128)}, f32[8,16,512]{2,1,0:T(8,128)S(1)}, s32[8]{0:T(128)S(1)}, f32[16,6144]{1,0:T(8,128)S(1)}, f32[3,6144]{1,0:T(4,128)S(1)}, /*index=5*/...) while((s32[]{:T(128)}, f32[8,16,512]{2,1,0:T(8,128)S(1)}, ...), condition=%wide.region_7.8_spmd, body=%wide.region_6.7_spmd.sunk | while | flops 246620224 | bytes 1092197 | solution.py:58
  871.3 1.0 copy-done.4
  872.7 45.1 %all-gather.2.cloned.1.call-done = f32[5,32,4096]{2,1,0:T(8,128)} async-done(((f32[5,16,4096]{2,1,0:T(8,128)}), f32[5,32,4096]{2,1,0:T(8,128)}) %all-gather.2.cloned.1.call-update) | async-done | bytes 2621456 | tf_op jit(solution)/shard_map/all_gather | solution.py:117
  917.8 5.6 fusion.2577
  923.9 1.3 copy-done.1
  925.2 1.6 bitcast_add_fusion
  926.8 1122.0 %all-reduce.2.cloned.1.call-done = f32[160,160]{0,1:T(8,128)} async-done(((f32[160,160]{0,1:T(8,128)}), f32[160,160]{0,1:T(8,128)}) %all-reduce.2.cloned.1.call-update) | async-done | bytes 102416 | tf_op jit(solution)/shard_map/psum | solution.py:119
  2049.9 11.7 cholesky.44
  2062.9 9.8 custom-call.10
  2074.0 12.0 cholesky.55
  2087.3 9.8 custom-call.11
  2097.8 2.7 fusion.2532
  2100.6 1.0 copy.29
  2101.6 1.1 convolution_bitcast_fusion.1
  2102.7 1.2 convolution_bitcast_fusion
  2103.9 2.0 copy.30
  2105.9 1.0 copy.28
  (952 shorter events, 424.7 us)
Async XLA Ops:
  7.2 910.6 %all-gather.2.cloned.1.call-start = ((), (), s32[]{:S(2)}) async-start(), calls=%async_computation | async-start | bytes 3932160 | tf_op jit(solution)/shard_map/all_gather | solution.py:117
  8.1 17.2 collective-permute-start.2
  10.3 15.0 collective-permute-start.3
  16.8 8.5 collective-permute-start
  16.9 8.4 collective-permute-start.1
  25.4 206.0 %copy-start.3 = (f32[16,1,4096]{2,1,0:T(1,128)S(1)}, f32[16,1,4096]{2,1,0:T(1,128)}, u32[]{:S(2)}) copy-start(f32[16,1,4096]{2,1,0:T(1,128)} %param.13) | copy-start | bytes 786436
  231.6 8.2 collective-permute-start.4
  231.9 7.9 collective-permute-start.5
  442.7 8.0 collective-permute-start.6
  442.8 8.0 collective-permute-start.7
  654.8 8.4 collective-permute-start.8
  656.7 6.6 collective-permute-start.9
  871.3 1.1 copy-start.4
  872.4 1176.4 %all-reduce.2.cloned.1.call-start = ((), (), s32[]{:S(2)}) async-start(), calls=%async_computation.1 | async-start | bytes 327680 | tf_op jit(solution)/shard_map/psum | solution.py:119
  917.8 5.6 copy-start
  923.9 1.3 copy-start.1
  2073.9 27.7 %copy-start.2 = (f32[4,32,4096]{2,1,0:T(8,128)S(1)}, f32[4,32,4096]{2,1,0:T(8,128)}, u32[]{:S(2)}) copy-start(f32[4,32,4096]{2,1,0:T(8,128)} %copy-done.1) | copy-start | bytes 6291460
Sparse Core Ops, SparseCore 0:
  872.5 45.1 all-gather.1
  923.5 1125.2 all-reduce.1
where the time goes:
time: 2130 us; the launch traced here: 2110 us
  waiting for transfers between devices  1170 us (55%)
  loops' own time  407 us (19%)
  matrix products  296 us (14%)
  local copies, waits for them, and re-layouts  140 us (7%)
  other arithmetic  51.7 us (2%)
  starting transfers between devices  32 us (2%)
    psum x1, waiting for transfers between devices, local(): gram = lax.psum(row_products(flat), ('blk', 'leaf'))  1120 us
    another operation x4, loops' own time, band_product(): lax.scan(turn, jnp.zeros((), jnp.int32), jnp.arange(8, dtype=jnp.int32))  407 us
    dot_general x576, matrix products, turn(): total = total + jnp.dot(near_field, tile, precision=exact)  284 us
    dynamic_slice x160, local copies, waits for them, and re-layouts, turn(): listed = lax.dynamic_index_in_dim(weights[offset], block, 0, False)  105 us
    all_gather x1, waiting for transfers between devices, local(): whole = lax.all_gather(half_panel, 'rhs', axis=1, tiled=True)  45.1 us
  transfers between devices with their start and end apart: 12, of which 7 were waited for; matrix products, arithmetic and copies ran while one was open for 0% of the time, Pallas kernels for 0%

commit v1 on v0

--- a/solution.py
+++ b/solution.py
@@ -11,6 +11,19 @@
 centre_shift = 1.5
 amplitude = 1.1
 exact = lax.Precision.HIGHEST
+
+
+def surface_report(inner_x):
+    block_out = jnp.concatenate(
+        lax.all_to_all(
+            jnp.stack([inner_x for _ in range(lax.axis_size("rhs"))], axis=0),
+            "rhs",
+            split_axis=0,
+            concat_axis=0,
+        ),
+        1,
+    )
+    return block_out
 
 
 def extended(x, sides, width):
@@ -114,7 +127,7 @@
     half_panel = jnp.stack(powers, axis=0)
     count_points = own_rows * lax.axis_size("blk") * lax.axis_size("leaf")
     sides_here = field.shape[0]
-    whole = lax.all_gather(half_panel, "rhs", axis=1, tiled=True)
+    whole = surface_report(half_panel)
     flat = whole.reshape(-1, own_rows)
     gram = lax.psum(row_products(flat), ("blk", "leaf"))
     inverse_low, combo = galerkin(gram, count_points, M)

time: 2130 us -> 2120 us (level)
    all_gather x1 -> x0, waiting for transfers between devices: 45.1 us -> none  [local(): whole = lax.all_gather(half_panel, 'rhs', axis=1, tiled=True)]
    all_to_all x0 -> x1, waiting for transfers between devices: none -> 24.5 us  [surface_report(): lax.all_to_all(jnp.stack([inner_x for _ in range(lax.axis_size('rhs'))],...]
where the time goes in v1:
time: 2120 us; the launch traced here: 2110 us
  waiting for transfers between devices  1150 us (54%)
  loops' own time  414 us (20%)
  matrix products  293 us (14%)
  local copies, waits for them, and re-layouts  142 us (7%)
  other arithmetic  53.5 us (3%)
  starting transfers between devices  37.4 us (2%)
    psum x1, waiting for transfers between devices, local(): gram = lax.psum(row_products(flat), ('blk', 'leaf'))  1120 us
    another operation x4, loops' own time, band_product(): lax.scan(turn, jnp.zeros((), jnp.int32), jnp.arange(8, dtype=jnp.int32))  414 us
    dot_general x576, matrix products, turn(): total = total + jnp.dot(near_field, tile, precision=exact)  284 us
    dynamic_slice x160, local copies, waits for them, and re-layouts, turn(): listed = lax.dynamic_index_in_dim(weights[offset], block, 0, False)  105 us
  transfers between devices with their start and end apart: 12, of which 7 were waited for; matrix products, arithmetic and copies ran while one was open for 0% of the time, Pallas kernels for 0%

profile of v1, /device:TPU:2, one launch (start us, length us, event | category | flops | bytes accessed | tf_op | source)
XLA Modules:
  0.0 2106.4 jit_solution(8245058204112714715)
XLA Ops:
  8.0 2.2 collective-permute-start.2
  10.2 5.4 collective-permute-start.3
  15.6 1.1 copy.50
  16.8 5.6 collective-permute-start.1
  22.4 1.1 bitcast_dynamic-update-slice_fusion
  25.3 209.2 %while.52 = (s32[]{:T(128)}, f32[8,16,512]{2,1,0:T(8,128)S(1)}, s32[8]{0:T(128)S(1)}, f32[16,6144]{1,0:T(8,128)S(1)}, f32[3,6144]{1,0:T(4,128)S(1)}, /*index=5*/...) while((s32[]{:T(128)}, f32[8,16,512]{2,1,0:T(8,128)S(1)}, ...), condition=%wide.region_1.2_spmd, body=%wide.region_0.1_spmd.sunk | while | flops 246620224 | bytes 1092197 | solution.py:71
  234.8 5.9 collective-permute-start.5
  241.1 1.6 collective-permute-done.4
  242.8 208.2 %while.53 = (s32[]{:T(128)}, f32[8,16,512]{2,1,0:T(8,128)S(1)}, s32[8]{0:T(128)S(1)}, f32[16,6144]{1,0:T(8,128)S(1)}, f32[3,6144]{1,0:T(4,128)S(1)}, /*index=5*/...) while((s32[]{:T(128)}, f32[8,16,512]{2,1,0:T(8,128)S(1)}, ...), condition=%wide.region_3.4_spmd, body=%wide.region_2.3_spmd.sunk | while | flops 246620224 | bytes 1092197 | solution.py:71
  451.2 6.4 collective-permute-start.7
  457.8 1.5 collective-permute-done.6
  459.5 205.4 %while.54 = (s32[]{:T(128)}, f32[8,16,512]{2,1,0:T(8,128)S(1)}, s32[8]{0:T(128)S(1)}, f32[16,6144]{1,0:T(8,128)S(1)}, f32[3,6144]{1,0:T(4,128)S(1)}, /*index=5*/...) while((s32[]{:T(128)}, f32[8,16,512]{2,1,0:T(8,128)S(1)}, ...), condition=%wide.region_5.6_spmd, body=%wide.region_4.5_spmd.sunk | while | flops 246620224 | bytes 1092197 | solution.py:71
  665.0 1.8 collective-permute-start.8
  666.8 4.5 collective-permute-start.9
  671.6 1.8 collective-permute-done.8
  673.5 205.9 %while.55 = (s32[]{:T(128)}, f32[8,16,512]{2,1,0:T(8,128)S(1)}, s32[8]{0:T(128)S(1)}, f32[16,6144]{1,0:T(8,128)S(1)}, f32[3,6144]{1,0:T(4,128)S(1)}, /*index=5*/...) while((s32[]{:T(128)}, f32[8,16,512]{2,1,0:T(8,128)S(1)}, ...), condition=%wide.region_7.8_spmd, body=%wide.region_6.7_spmd.sunk | while | flops 246620224 | bytes 1092197 | solution.py:71
  879.7 1.7 pad_maximum_fusion
  881.4 5.1 all-to-all-start
  886.8 24.5 %all-to-all-done = f32[2,5,16,4096]{3,2,1,0:T(8,128)S(1)} async-done(((f32[2,5,16,4096]{3,2,1,0:T(8,128)}), f32[2,5,16,4096]{3,2,1,0:T(8,128)S(1)}, u32[]{:S(2)}, u32[]{:S(2)}) %all-to-all-start) | async-done | bytes 2621472 | tf_op jit(solution)/shard_map/all_to_all | solution.py:18
  911.5 2.6 fusion.2570
  914.1 2.9 fusion.2577
  917.2 1.4 copy-done
  918.8 1.6 bitcast_add_fusion
  920.4 1120.6 %all-reduce.2.cloned.1.call-done = f32[160,160]{0,1:T(8,128)} async-done(((f32[160,160]{0,1:T(8,128)}), f32[160,160]{0,1:T(8,128)}) %all-reduce.2.cloned.1.call-update) | async-done | bytes 102416 | tf_op jit(solution)/shard_map/psum | solution.py:132
  2042.1 11.7 cholesky.44
  2055.2 9.8 custom-call.10
  2066.2 12.0 cholesky.55
  2079.5 9.8 custom-call.11
  2090.1 2.7 fusion.2532
  2093.8 1.1 convolution_bitcast_fusion.1
  2094.9 1.2 convolution_bitcast_fusion
  2096.1 2.0 copy.33
  (951 shorter events, 427.2 us)
Async XLA Ops:
  8.0 17.2 collective-permute-start.2
  10.2 15.0 collective-permute-start.3
  16.7 8.5 collective-permute-start
  16.8 8.4 collective-permute-start.1
  25.3 209.2 %copy-start.2 = (f32[16,1,4096]{2,1,0:T(1,128)S(1)}, f32[16,1,4096]{2,1,0:T(1,128)}, u32[]{:S(2)}) copy-start(f32[16,1,4096]{2,1,0:T(1,128)} %param.13) | copy-start | bytes 786436
  234.7 8.0 collective-permute-start.4
  234.8 7.9 collective-permute-start.5
  451.1 8.2 collective-permute-start.6
  451.2 8.3 collective-permute-start.7
  665.0 8.4 collective-permute-start.8
  666.8 6.6 collective-permute-start.9
  881.4 29.8 %all-to-all-start = ((f32[2,5,16,4096]{3,2,1,0:T(8,128)}), f32[2,5,16,4096]{3,2,1,0:T(8,128)S(1)}, u32[]{:S(2)}, u32[]{:S(2)}) async-start(f32[2,5,16,4096]{3,2,1,0:T(8,128)} %pad_maximum_fusion), calls=%async_computation | async-start | bytes 5242880 | tf_op jit(solution)/shard_map/all_to_all | solution.py:18
  886.6 1154.5 %all-reduce.2.cloned.1.call-start = ((), (), s32[]{:S(2)}) async-start(), calls=%async_computation.1 | async-start | bytes 327680 | tf_op jit(solution)/shard_map/psum | solution.py:132
  914.1 2.9 copy-start.1
  917.0 1.6 copy-start
Sparse Core Ops, SparseCore 0:
  917.1 1123.8 all-reduce.1
